TPU v7x, 32 devices: a whole 2x2x4 slice. The times are simulated.
32 devices in a mesh: groups: 2 (over y), blk: 4 (over z), oct: 2 (over x), sub: 2 (over core).
Axes of the slice: x: 2, y: 2, z: 4, core: 2. Of those that a mesh axis runs over, the one named last changes fastest.
Arguments:
- positions: float32 [3, 65536], P(None, ('groups', 'blk', 'oct', 'sub')), parts along dimension 1, may hold values from 0 to 320
- polarizability: float32 [65536], P(('groups', 'blk', 'oct', 'sub')), parts along dimension 0, may hold values from 0.5 to 1.5
- permanent_field: float32 [3, 65536], P(None, ('groups', 'blk', 'oct', 'sub')), parts along dimension 1, may hold values from -40 to 40
- group_id: int32 [65536], P(('groups', 'blk', 'oct', 'sub')), parts along dimension 0, may hold values from 0 to 10921, never falling along the last dimension, each value on 1 to 6 neighbouring positions
- pair_mask: int32 [512, 9], P(('groups', 'blk', 'oct', 'sub')), parts along dimension 0, may hold values from 0 to 1, as said below
Outputs:
- dipoles: float32 [3, 65536], P(None, ('groups', 'blk', 'oct', 'sub')), parts along dimension 1
- residual: float32 [3, 65536], P(None, ('groups', 'blk', 'oct', 'sub')), parts along dimension 1
There are 2 independent parts, one for each index of `groups`. A program takes and returns all parts, laid end to end along the dimension named above; each array names one. Nothing has to cross between parts.
Inputs may be any that keep to these rules, and one draw needn't show every extreme that they name: `group_id`: never falls from one atom to the next; each value names 1 to 6 consecutive atoms. pair_mask[b, 4] = 1, and pair_mask[b, 4 + o] = pair_mask[(b + o) mod 256, 4 - o].
All inputs are finite; a program needn't handle non-finite values.
Results may differ from a plain program's by a relative error of at most 0.0003.
Values sent between devices are 32-bit elements; how exact they have to be, the bound alone decides.
No kernel may reach another device: no remote copies, remote signals or barrier semaphores. Data moves between devices by JAX's collectives and lax.ppermute only.
A program may use at most 64 MiB of HBM per device.

v0:
```python
import math
import jax
import jax.numpy as jnp
import numpy as np
from jax import lax
from jax.sharding import PartitionSpec as P

BOXES_DEV = 2
BLOCK = 128
ORDER = 5
NODE_PAD = 128
ITERS = 2
side_length = 32.0
layer_gap = 2.5
thole_damp = 0.39
highest = lax.Precision.HIGHEST


def padded(cells, sides, width):
    for axis, dim in sides:
        count = lax.axis_size(axis)
        head = lax.slice_in_dim(cells, 0, width, axis=dim)
        tail = lax.slice_in_dim(cells, cells.shape[dim] - width, cells.shape[dim], axis=dim)
        cells = jnp.concatenate(
            [
                lax.ppermute(tail, axis, [(i, (i + 1) % count) for i in range(count)]),
                cells,
                lax.ppermute(head, axis, [((i + 1) % count, i) for i in range(count)]),
            ],
            axis=dim,
        )
    return cells


def wrap_image(delta, period):
    return delta - period * jnp.floor(delta / period + 0.5)


def split_size(total, limit):
    best = 1
    for factor in range(1, min(total, limit) + 1):
        if total % factor == 0:
            best = factor
    return best


def near_tiles(target, source, moments, keep_tile, length_z):
    delta_x = wrap_image(target[0][:, :, None] - source[0][:, None, :], side_length)
    delta_y = wrap_image(target[1][:, :, None] - source[1][:, None, :], side_length)
    delta_z = wrap_image(target[2][:, :, None] - source[2][:, None, :], length_z)
    keep = (keep_tile[:, None, None] > 0.5) & (target[4][:, :, None] != source[4][:, None, :])
    dist_sq = jnp.where(keep, delta_x * delta_x + delta_y * delta_y + delta_z * delta_z, 1.0)
    inv_three = lax.rsqrt(dist_sq) / dist_sq
    scaled = (
        thole_damp
        * dist_sq
        * jnp.sqrt(dist_sq)
        * lax.rsqrt(target[3][:, :, None] * source[3][:, None, :])
    )
    lam_three = -jnp.expm1(-scaled)
    lam_five = lam_three - scaled * jnp.exp(-scaled)
    coef_five = jnp.where(keep, 3.0 * lam_five * inv_three / dist_sq, 0.0)
    coef_three = jnp.where(keep, lam_three * inv_three, 0.0)
    along = (
        delta_x * moments[0][:, None, :]
        + delta_y * moments[1][:, None, :]
        + delta_z * moments[2][:, None, :]
    )
    weighted = coef_five * along
    field_x = jnp.sum(weighted * delta_x - coef_three * moments[0][:, None, :], axis=2)
    field_y = jnp.sum(weighted * delta_y - coef_three * moments[1][:, None, :], axis=2)
    field_z = jnp.sum(weighted * delta_z - coef_three * moments[2][:, None, :], axis=2)
    return jnp.stack([field_x, field_y, field_z])


def near_total(static_ext, dipole_ext, mask_rows, length_z, atom_count):
    reach = (mask_rows.shape[1] - 1) // 2
    width = reach * BLOCK
    blocks = atom_count // BLOCK
    target = static_ext[:, width : width + atom_count].reshape(5, blocks, BLOCK)
    total = jnp.zeros((3, blocks, BLOCK), static_ext.dtype)
    for offset in range(-reach, reach + 1):
        begin = (reach + offset) * BLOCK
        source = static_ext[:, begin : begin + atom_count].reshape(5, blocks, BLOCK)
        moments = dipole_ext[:, begin : begin + atom_count].reshape(3, blocks, BLOCK)
        keep_tile = mask_rows[:, reach + offset].astype(static_ext.dtype)
        total = total + near_tiles(target, source, moments, keep_tile, length_z)
    return total.reshape(3, atom_count)


def node_tables():
    count = ORDER
    roots = np.cos((2.0 * np.arange(count) + 1.0) * np.pi / (2.0 * count))
    degree = np.arange(count)
    coeff = (
        2.0 / count * np.cos(np.outer(2.0 * np.arange(count) + 1.0, degree) * np.pi / (2.0 * count))
    )
    coeff = np.where(degree[None, :] == 0, 1.0 / count, coeff)
    index = np.arange(NODE_PAD)
    live = index < count**3
    safe = np.where(live, index, 0)
    first = safe // (count * count)
    second = safe // count % count
    third = safe % count
    levels = np.arange(count)[None, :]
    pick_a = (first[:, None] == levels) * live[:, None] * 1.0
    pick_b = (second[:, None] == levels) * 1.0
    pick_c = (third[:, None] == levels) * 1.0
    node_x = 16.0 * (1.0 + roots[first])
    node_y = 16.0 * (1.0 + roots[second])
    node_t = roots[third]
    tables = [coeff, pick_a, pick_b, pick_c, node_x, node_y, node_t]
    return [jnp.asarray(item, jnp.float32) for item in tables]


def interpolation(coords, box_ids, box_height):
    coeff, pick_a, pick_b, pick_c, node_x, node_y, node_t = node_tables()
    scaled_x = coords[0] / 16.0 - 1.0
    scaled_y = coords[1] / 16.0 - 1.0
    scaled_z = (
        2.0 * (coords[2] - box_ids.astype(coords.dtype)[:, None] * box_height) / box_height - 1.0
    )

    def basis(values, picks):
        terms = [jnp.ones_like(values), values]
        for degree in range(2, ORDER):
            terms.append(2.0 * values * terms[-1] - terms[-2])
        stacked = jnp.stack(terms[:ORDER])
        smooth = jnp.einsum("kn,nba->kba", coeff, stacked, precision=highest)
        return jnp.einsum("pk,kba->pba", picks, smooth, precision=highest)

    return basis(scaled_x, pick_a) * basis(scaled_y, pick_b) * basis(scaled_z, pick_c)


def far_block(target_ids, source_ids, weights, slabs, box_height, length_z):
    coeff, pick_a, pick_b, pick_c, node_x, node_y, node_t = node_tables()
    height_t = (
        target_ids.astype(weights.dtype)[:, None] * box_height
        + 0.5 * box_height * (1.0 + node_t)[None, :]
    )
    height_s = (
        source_ids.astype(weights.dtype)[:, None] * box_height
        + 0.5 * box_height * (1.0 + node_t)[None, :]
    )
    delta_x = wrap_image(node_x[:, None] - node_x[None, :], side_length)[None, :, None, :]
    delta_y = wrap_image(node_y[:, None] - node_y[None, :], side_length)[None, :, None, :]
    delta_z = wrap_image(height_t[:, :, None, None] - height_s[None, None, :, :], length_z)
    apart = jnp.abs(target_ids[:, None] // BOXES_DEV - source_ids[None, :] // BOXES_DEV)
    apart = jnp.minimum(apart, slabs - apart)
    keep = (apart >= 1)[:, None, :, None]
    dist_sq = jnp.where(
        keep,
        delta_x * delta_x + delta_y * delta_y + delta_z * delta_z + box_height * box_height,
        1.0,
    )
    inv_three = lax.rsqrt(dist_sq) / dist_sq
    coef_five = jnp.where(keep, 3.0 * inv_three / dist_sq, 0.0)
    coef_three = jnp.where(keep, inv_three, 0.0)
    weight_x = weights[:, 0, :][None, None]
    weight_y = weights[:, 1, :][None, None]
    weight_z = weights[:, 2, :][None, None]
    weighted = coef_five * (delta_x * weight_x + delta_y * weight_y + delta_z * weight_z)
    field_x = jnp.sum(weighted * delta_x - coef_three * weight_x, axis=(2, 3))
    field_y = jnp.sum(weighted * delta_y - coef_three * weight_y, axis=(2, 3))
    field_z = jnp.sum(weighted * delta_z - coef_three * weight_z, axis=(2, 3))
    return jnp.stack([field_x, field_y, field_z], axis=1)


def on_device(positions, polarizability, permanent_field, group_id, pair_mask):
    slabs = lax.axis_size(("blk", "oct", "sub"))
    member = lax.axis_index(("blk", "oct", "sub"))
    atom_count = positions.shape[1]
    length_z = layer_gap * atom_count * slabs / 256.0
    box_height = length_z / (BOXES_DEV * slabs)
    per_box = atom_count // BOXES_DEV
    width = (pair_mask.shape[1] - 1) // 2 * BLOCK
    group_limit = max(1, 32 // BOXES_DEV)
    static = jnp.concatenate(
        [positions, polarizability[None, :], group_id.astype(jnp.float32)[None, :]], axis=0
    )
    static_ext = padded(static, ((("blk", "oct", "sub"), 1),), width)
    own_boxes = member * BOXES_DEV + jnp.arange(BOXES_DEV, dtype=jnp.int32)
    interp = interpolation(positions.reshape(3, BOXES_DEV, per_box), own_boxes, box_height)
    surface = 4.0 * math.pi / 3.0 / (side_length * side_length * length_z)

    def induced(dipoles, total):
        dipole_ext = padded(dipoles, ((("blk", "oct", "sub"), 1),), width)
        near = near_total(static_ext, dipole_ext, pair_mask, length_z, atom_count)
        weights = jnp.einsum(
            "pba,cba->bcp", interp, dipoles.reshape(3, BOXES_DEV, per_box), precision=highest
        )
        piece = lax.all_gather(weights, ("blk", "oct", "sub"), axis=0, tiled=True)
        start = jnp.int32(0)
        count = piece.shape[0]
        size = split_size(count, group_limit)
        grouped = piece.reshape(count // size, size, 3, piece.shape[2])

        def visit(acc, item):
            index, bundle = item
            sources = start + index * size + jnp.arange(size, dtype=jnp.int32)
            return (acc + far_block(own_boxes, sources, bundle, slabs, box_height, length_z), None)

        result, unused = lax.scan(
            visit, jnp.zeros_like(weights), (jnp.arange(count // size, dtype=jnp.int32), grouped)
        )
        far = jnp.einsum("pba,bcp->cba", interp, result, precision=highest).reshape(3, atom_count)
        return near + far - surface * total[:, None]

    def moment(values):
        return lax.psum(jnp.sum(values, axis=1), ("blk", "oct", "sub"))

    def squares(resid, scaled):
        return lax.psum(jnp.sum(resid * scaled), ("blk", "oct", "sub"))

    dipoles = polarizability[None, :] * permanent_field
    residual = induced(dipoles, moment(dipoles))
    precond = polarizability[None, :] * residual
    direction = precond
    norm_now = squares(residual, precond)
    for step in range(ITERS):
        image = direction / polarizability[None, :] - induced(direction, moment(direction))
        rate = norm_now / lax.psum(jnp.sum(direction * image), ("blk", "oct", "sub"))
        dipoles = dipoles + rate * direction
        residual = residual - rate * image
        if step + 1 < ITERS:
            precond = polarizability[None, :] * residual
            norm_next = squares(residual, precond)
            direction = precond + norm_next / norm_now * direction
            norm_now = norm_next
    return (dipoles, residual)


def solution(mesh):
    return jax.shard_map(
        on_device,
        mesh=mesh,
        in_specs=(
            P(None, ("groups", "blk", "oct", "sub")),
            P(("groups", "blk", "oct", "sub")),
            P(None, ("groups", "blk", "oct", "sub")),
            P(("groups", "blk", "oct", "sub")),
            P(("groups", "blk", "oct", "sub"), None),
        ),
        out_specs=(
            P(None, ("groups", "blk", "oct", "sub")),
            P(None, ("groups", "blk", "oct", "sub")),
        ),
        check_vma=False,
    )
```

profile of v0, /device:TPU:0, one launch (start us, length us, event | category | flops | bytes accessed | tf_op | source)
XLA Modules:
  0.0 428.3 jit_solution(15247812564218952183)
XLA Ops:
  2.6 5.0 %collective-permute-start.2 = (f32[5,512]{1,0:T(8,128)S(1)}, f32[5,512]{1,0:T(8,128)S(1)}, u32[]{:S(2)}, u32[]{:S(2)}) collective-permute-start(f32[5,512]{1,0:T(8,128)S(1)} %get-tuple-element.990), channel_id=1, source_target_pairs={{1,0},{2,1},{3,2},{4,3},{5,4},{6,5},{7,6},{8,7},{9,8},{10,9},{11,1... | collective-permute-start | bytes 30728 | tf_op jit(solution)/shard_map/ppermute | solution.py:28
  8.6 4.4 %collective-permute-start.3 = (f32[3,512]{1,0:T(4,128)S(1)}, f32[3,512]{1,0:T(4,128)S(1)}, u32[]{:S(2)}, u32[]{:S(2)}) collective-permute-start(f32[3,512]{1,0:T(4,128)S(1)} %get-tuple-element.1086), channel_id=1, source_target_pairs={{1,0},{2,1},{3,2},{4,3},{5,4},{6,5},{7,6},{8,7},{9,8},{10,9},{11,1... | collective-permute-start | bytes 18440 | tf_op jit(solution)/shard_map/ppermute | solution.py:28
  14.0 29.5 %psum.49 = f32[3]{0:T(128)S(1)} all-reduce(f32[3]{0:T(128)S(1)} %get-tuple-element.927), channel_id=1, replica_groups=mesh['groups'=2,'blk'=4,'oct'=2,'sub'=2] {'blk','oct','sub'}, use_global_device_ids=true, to_apply=%region_33.34 | all-reduce | flops 3 | bytes 24 | tf_op jit(solution)/shard_map/psum | solution.py:210
  47.7 1.8 convolution_multiply_fusion.1
  49.6 1.8 fusion.90
  52.0 17.8 %all_gather.9 = f32[32,3,128]{2,1,0:T(4,128)S(1)} all-gather(f32[2,3,128]{2,1,0:T(4,128)S(1)} %fusion.782), channel_id=1, replica_groups=mesh['groups'=2,'blk'=4,'oct'=2,'sub'=2] {'blk','oct','sub'}, dimensions={0}, use_global_device_ids=true | all-gather | bytes 52224 | tf_op jit(solution)/shard_map/all_gather | solution.py:192
  69.9 13.5 %while.51 = (s32[]{:T(128)}, f32[2,3,128]{2,0,1:T(2,128)S(1)}, s32[2]{0:T(128)S(1)}, f32[2,16,3,128]{3,1,2,0:T(8,128)S(1)}, s32[]{:T(128)}, /*index=5*/s32[]{:T(...) while((s32[]{:T(128)}, f32[2,3,128]{2,0,1:T(2,128)S(1)}, ...), condition=%wide.region_31.32_spmd.clone.clone.clone.clone, body=%wide.region_27.31_spmd.sunk.clone.clone.clone.clone.sunk | while | flops 16765948 | bytes 2795035 | solution.py:203
  71.8 4.8 %subtract_reduce_fusion.9 = (f32[2,128]{1,0:T(2,128)S(1)}, f32[2,128]{1,0:T(2,128)S(1)}, f32[2,128]{1,0:T(2,128)S(1)}) fusion(f32[16,128]{1,0:T(8,128)S(1)} %get-tuple-element.1216, f32[128,128]{1,0:T(8,128)S(1)} %get-tuple-element.1217, pred[2,16]{1,0:T(4,128)(4,1)S(1)} %fusion.814, f32[16,128]{1,0:T(8,128)S(1)} %broadcast_add_fusion.12, ...), kind=kLoop, calls=%fused_computation.28.clone.1 | loop fusion | flops 15727872 | bytes 1282080 | tf_op jit(solution)/shard_map/while/body/eval_jaxpr/reduce_sum | solution.py:163
  78.5 4.8 %subtract_reduce_fusion.9 = (f32[2,128]{1,0:T(2,128)S(1)}, f32[2,128]{1,0:T(2,128)S(1)}, f32[2,128]{1,0:T(2,128)S(1)}) fusion(f32[16,128]{1,0:T(8,128)S(1)} %get-tuple-element.1216, f32[128,128]{1,0:T(8,128)S(1)} %get-tuple-element.1217, pred[2,16]{1,0:T(4,128)(4,1)S(1)} %fusion.814, f32[16,128]{1,0:T(8,128)S(1)} %broadcast_add_fusion.12, ...), kind=kLoop, calls=%fused_computation.28.clone.1 | loop fusion | flops 15727872 | bytes 1282080 | tf_op jit(solution)/shard_map/while/body/eval_jaxpr/reduce_sum | solution.py:163
  84.2 4.0 fusion.558
  88.2 4.0 fusion.585
  92.2 4.0 fusion.567
  96.2 4.0 fusion.576
  100.2 4.0 fusion.603
  104.2 4.0 fusion.621
  108.2 4.0 fusion.612
  112.2 7.3 %fusion.630 = (f32[16,128]{1,0:T(8,128)S(1)}, f32[16,128]{1,0:T(8,128)S(1)}, f32[16,128]{1,0:T(8,128)S(1)}, f32[16,128]{1,0:T(8,128)S(1)}, f32[16,128]{1,0:T(8,128)S(1)}, /*index=5*/f32[16,128]{1,0:T(8,128)S(1)}) fusion(f32[16,128]{1,0:T(8,128)S(1)} %bitcast.840, f32[16,128]{1,0:T(8,128)S(1)} %bitcast.735, f32[16,128]{1,0:T(8,128)S(1)} %bitcast.931, ...), kind=kLoop, calls=%fused_computation.815 | loop fusion | flops 30920704 | bytes 180256 | tf_op jit(solution)/shard_map/reduce_sum | solution.py:70
  120.7 31.6 %psum.51 = f32[3]{0:T(128)S(1)} all-reduce(f32[3]{0:T(128)S(1)} %get-tuple-element.923), channel_id=1, replica_groups=mesh['groups'=2,'blk'=4,'oct'=2,'sub'=2] {'blk','oct','sub'}, use_global_device_ids=true, to_apply=%region_69.70 | all-reduce | flops 3 | bytes 24 | tf_op jit(solution)/shard_map/psum | solution.py:210
  153.2 4.4 %collective-permute-start.5 = (f32[3,512]{1,0:T(4,128)S(1)}, f32[3,512]{1,0:T(4,128)S(1)}, u32[]{:S(2)}, u32[]{:S(2)}) collective-permute-start(f32[3,512]{1,0:T(4,128)S(1)} %get-tuple-element.1078), channel_id=1, source_target_pairs={{1,0},{2,1},{3,2},{4,3},{5,4},{6,5},{7,6},{8,7},{9,8},{10,9},{11,1... | collective-permute-start | bytes 18440 | tf_op jit(solution)/shard_map/ppermute | solution.py:28
  157.6 17.3 %all_gather.10 = f32[32,3,128]{2,1,0:T(4,128)S(1)} all-gather(f32[2,3,128]{2,1,0:T(4,128)S(1)} %fusion.684), channel_id=1, replica_groups=mesh['groups'=2,'blk'=4,'oct'=2,'sub'=2] {'blk','oct','sub'}, dimensions={0}, use_global_device_ids=true | all-gather | bytes 52224 | tf_op jit(solution)/shard_map/all_gather | solution.py:192
  174.9 13.0 %while.52 = (s32[]{:T(128)}, f32[2,3,128]{2,0,1:T(2,128)S(1)}, s32[2]{0:T(128)S(1)}, f32[2,16,3,128]{3,1,2,0:T(8,128)S(1)}, s32[]{:T(128)}, /*index=5*/s32[]{:T(...) while((s32[]{:T(128)}, f32[2,3,128]{2,0,1:T(2,128)S(1)}, ...), condition=%wide.region_67.68_spmd.clone.clone.clone.clone, body=%wide.region_63.67_spmd.sunk.clone.clone.clone.clone.sunk | while | flops 16765948 | bytes 2795035 | solution.py:203
  176.6 4.8 %subtract_reduce_fusion.10 = (f32[2,128]{1,0:T(2,128)S(1)}, f32[2,128]{1,0:T(2,128)S(1)}, f32[2,128]{1,0:T(2,128)S(1)}) fusion(f32[16,128]{1,0:T(8,128)S(1)} %get-tuple-element.1230, f32[128,128]{1,0:T(8,128)S(1)} %get-tuple-element.1231, pred[2,16]{1,0:T(4,128)(4,1)S(1)} %fusion.817, f32[16,128]{1,0:T(8,128)S(1)} %broadcast_add_fusion.14, ...), kind=kLoop, calls=%fused_computation.82.clone.1 | loop fusion | flops 15727872 | bytes 1282080 | tf_op jit(solution)/shard_map/while/body/eval_jaxpr/reduce_sum | solution.py:163
  183.1 4.8 %subtract_reduce_fusion.10 = (f32[2,128]{1,0:T(2,128)S(1)}, f32[2,128]{1,0:T(2,128)S(1)}, f32[2,128]{1,0:T(2,128)S(1)}) fusion(f32[16,128]{1,0:T(8,128)S(1)} %get-tuple-element.1230, f32[128,128]{1,0:T(8,128)S(1)} %get-tuple-element.1231, pred[2,16]{1,0:T(4,128)(4,1)S(1)} %fusion.817, f32[16,128]{1,0:T(8,128)S(1)} %broadcast_add_fusion.14, ...), kind=kLoop, calls=%fused_computation.82.clone.1 | loop fusion | flops 15727872 | bytes 1282080 | tf_op jit(solution)/shard_map/while/body/eval_jaxpr/reduce_sum | solution.py:163
  188.0 4.0 fusion.602
  192.0 4.0 fusion.575
  196.1 4.0 fusion.566
  200.1 4.0 fusion.557
  204.1 4.0 fusion.584
  208.1 4.0 fusion.611
  212.1 4.0 fusion.620
  216.1 7.3 %fusion.629 = (f32[16,128]{1,0:T(8,128)S(1)}, f32[16,128]{1,0:T(8,128)S(1)}, f32[16,128]{1,0:T(8,128)S(1)}, f32[16,128]{1,0:T(8,128)S(1)}, f32[16,128]{1,0:T(8,128)S(1)}, /*index=5*/f32[16,128]{1,0:T(8,128)S(1)}) fusion(f32[16,128]{1,0:T(8,128)S(1)} %bitcast.872, f32[16,128]{1,0:T(8,128)S(1)} %bitcast.736, f32[16,128]{1,0:T(8,128)S(1)} %bitcast.939, ...), kind=kLoop, calls=%fused_computation.814 | loop fusion | flops 30920704 | bytes 180256 | tf_op jit(solution)/shard_map/reduce_sum | solution.py:70
  225.1 32.1 %all-reduce = (f32[]{:T(128)}, f32[]{:T(128)}) all-reduce(f32[]{:T(128)} %get-tuple-element.870, f32[]{:T(128)} %get-tuple-element.869), channel_id=1, replica_groups=mesh['groups'=2,'blk'=4,'oct'=2,'sub'=2] {'blk','oct','sub'}, use_global_device_ids=true, to_apply=%region_35.36 | all-reduce | flops 2 | bytes 16 | tf_op jit(solution)/shard_map/psum | solution.py:213
  259.1 30.1 %psum.53 = f32[]{:T(128)} all-reduce(f32[]{:T(128)} %fusion.632), channel_id=1, replica_groups=mesh['groups'=2,'blk'=4,'oct'=2,'sub'=2] {'blk','oct','sub'}, use_global_device_ids=true, to_apply=%region_73.74 | all-reduce | flops 1 | bytes 8 | tf_op jit(solution)/shard_map/psum | solution.py:213
  290.6 29.7 %psum.54 = f32[3]{0:T(128)S(1)} all-reduce(f32[3]{0:T(128)S(1)} %get-tuple-element.918), channel_id=1, replica_groups=mesh['groups'=2,'blk'=4,'oct'=2,'sub'=2] {'blk','oct','sub'}, use_global_device_ids=true, to_apply=%region_107.108 | all-reduce | flops 3 | bytes 24 | tf_op jit(solution)/shard_map/psum | solution.py:210
  321.3 4.4 %collective-permute-start.7 = (f32[3,512]{1,0:T(4,128)S(1)}, f32[3,512]{1,0:T(4,128)S(1)}, u32[]{:S(2)}, u32[]{:S(2)}) collective-permute-start(f32[3,512]{1,0:T(4,128)S(1)} %get-tuple-element.1070), channel_id=1, source_target_pairs={{1,0},{2,1},{3,2},{4,3},{5,4},{6,5},{7,6},{8,7},{9,8},{10,9},{11,1... | collective-permute-start | bytes 18440 | tf_op jit(solution)/shard_map/ppermute | solution.py:28
  325.7 17.3 %all_gather.11 = f32[32,3,128]{2,1,0:T(4,128)S(1)} all-gather(f32[2,3,128]{2,1,0:T(4,128)S(1)} %fusion.783), channel_id=1, replica_groups=mesh['groups'=2,'blk'=4,'oct'=2,'sub'=2] {'blk','oct','sub'}, dimensions={0}, use_global_device_ids=true | all-gather | bytes 52224 | tf_op jit(solution)/shard_map/all_gather | solution.py:192
  343.0 13.0 %while.53 = (s32[]{:T(128)}, f32[2,3,128]{2,0,1:T(2,128)S(1)}, s32[2]{0:T(128)S(1)}, f32[2,16,3,128]{3,1,2,0:T(8,128)S(1)}, s32[]{:T(128)}, /*index=5*/s32[]{:T(...) while((s32[]{:T(128)}, f32[2,3,128]{2,0,1:T(2,128)S(1)}, ...), condition=%wide.region_105.106_spmd.clone.clone.clone.clone, body=%wide.region_101.105_spmd.sunk.clone.clone.clone.clone.sunk | while | flops 16765948 | bytes 2795035 | solution.py:203
  344.7 4.8 %subtract_reduce_fusion.11 = (f32[2,128]{1,0:T(2,128)S(1)}, f32[2,128]{1,0:T(2,128)S(1)}, f32[2,128]{1,0:T(2,128)S(1)}) fusion(f32[16,128]{1,0:T(8,128)S(1)} %get-tuple-element.1244, f32[128,128]{1,0:T(8,128)S(1)} %get-tuple-element.1245, pred[2,16]{1,0:T(4,128)(4,1)S(1)} %fusion.820, f32[16,128]{1,0:T(8,128)S(1)} %broadcast_add_fusion.16, ...), kind=kLoop, calls=%fused_computation.136.clone.1 | loop fusion | flops 15727872 | bytes 1282080 | tf_op jit(solution)/shard_map/while/body/eval_jaxpr/reduce_sum | solution.py:163
  351.2 4.8 %subtract_reduce_fusion.11 = (f32[2,128]{1,0:T(2,128)S(1)}, f32[2,128]{1,0:T(2,128)S(1)}, f32[2,128]{1,0:T(2,128)S(1)}) fusion(f32[16,128]{1,0:T(8,128)S(1)} %get-tuple-element.1244, f32[128,128]{1,0:T(8,128)S(1)} %get-tuple-element.1245, pred[2,16]{1,0:T(4,128)(4,1)S(1)} %fusion.820, f32[16,128]{1,0:T(8,128)S(1)} %broadcast_add_fusion.16, ...), kind=kLoop, calls=%fused_computation.136.clone.1 | loop fusion | flops 15727872 | bytes 1282080 | tf_op jit(solution)/shard_map/while/body/eval_jaxpr/reduce_sum | solution.py:163
  356.1 4.0 fusion.556
  360.1 4.0 fusion.601
  364.2 4.0 fusion.565
  368.2 4.0 fusion.574
  372.2 4.0 fusion.583
  376.2 4.0 fusion.610
  380.3 4.0 fusion.619
  384.3 7.3 %fusion.628 = (f32[16,128]{1,0:T(8,128)S(1)}, f32[16,128]{1,0:T(8,128)S(1)}, f32[16,128]{1,0:T(8,128)S(1)}, f32[16,128]{1,0:T(8,128)S(1)}, f32[16,128]{1,0:T(8,128)S(1)}, /*index=5*/f32[16,128]{1,0:T(8,128)S(1)}) fusion(f32[16,128]{1,0:T(8,128)S(1)} %bitcast.862, f32[16,128]{1,0:T(8,128)S(1)} %bitcast.737, f32[16,128]{1,0:T(8,128)S(1)} %bitcast.947, ...), kind=kLoop, calls=%fused_computation.813 | loop fusion | flops 30920704 | bytes 180256 | tf_op jit(solution)/shard_map/reduce_sum | solution.py:70
  393.2 32.0 %psum.55 = f32[]{:T(128)} all-reduce(f32[]{:T(128)} %get-tuple-element.1104), channel_id=1, replica_groups=mesh['groups'=2,'blk'=4,'oct'=2,'sub'=2] {'blk','oct','sub'}, use_global_device_ids=true, to_apply=%region_109.110 | all-reduce | flops 1 | bytes 8 | tf_op jit(solution)/shard_map/psum | solution.py:222
  (174 shorter events, 24.9 us)
Async XLA Ops:
  0.6 45.0 %copy-start.8 = (f32[5,5,1]{1,0,2:T(8,128)S(1)}, f32[5,5,1]{1,0,2:T(8,128)}, u32[]{:S(2)}) copy-start(f32[5,5,1]{1,0,2:T(8,128)} %constant.532) | copy-start | bytes 304
  0.6 45.2 %copy-start.11 = (f32[128,5,1]{0,1,2:T(8,128)S(1)}, f32[128,5,1]{0,1,2:T(8,128)}, u32[]{:S(2)}) copy-start(f32[128,5,1]{0,1,2:T(8,128)} %constant.533) | copy-start | bytes 7684
  2.1 81.8 %collective-permute-start = (f32[5,512]{1,0:T(8,128)S(1)}, f32[5,512]{1,0:T(8,128)S(1)}, u32[]{:S(2)}, u32[]{:S(2)}) collective-permute-start(f32[5,512]{1,0:T(8,128)S(1)} %get-tuple-element.989), channel_id=1, source_target_pairs={{0,1},{1,2},{2,3},{3,4},{4,5},{5,6},{6,7},{7,8},{8,9},{9,10},{10,1... | collective-permute-start | bytes 30728 | tf_op jit(solution)/shard_map/ppermute | solution.py:26
  2.6 81.3 %collective-permute-start.2 = (f32[5,512]{1,0:T(8,128)S(1)}, f32[5,512]{1,0:T(8,128)S(1)}, u32[]{:S(2)}, u32[]{:S(2)}) collective-permute-start(f32[5,512]{1,0:T(8,128)S(1)} %get-tuple-element.990), channel_id=1, source_target_pairs={{1,0},{2,1},{3,2},{4,3},{5,4},{6,5},{7,6},{8,7},{9,8},{10,9},{11,1... | collective-permute-start | bytes 30728 | tf_op jit(solution)/shard_map/ppermute | solution.py:28
  8.6 75.2 %collective-permute-start.1 = (f32[3,512]{1,0:T(4,128)S(1)}, f32[3,512]{1,0:T(4,128)S(1)}, u32[]{:S(2)}, u32[]{:S(2)}) collective-permute-start(f32[3,512]{1,0:T(4,128)S(1)} %get-tuple-element.1085), channel_id=1, source_target_pairs={{0,1},{1,2},{2,3},{3,4},{4,5},{5,6},{6,7},{7,8},{8,9},{9,10},{10,1... | collective-permute-start | bytes 18440 | tf_op jit(solution)/shard_map/ppermute | solution.py:26
  8.6 75.2 %collective-permute-start.3 = (f32[3,512]{1,0:T(4,128)S(1)}, f32[3,512]{1,0:T(4,128)S(1)}, u32[]{:S(2)}, u32[]{:S(2)}) collective-permute-start(f32[3,512]{1,0:T(4,128)S(1)} %get-tuple-element.1086), channel_id=1, source_target_pairs={{1,0},{2,1},{3,2},{4,3},{5,4},{6,5},{7,6},{8,7},{9,8},{10,9},{11,1... | collective-permute-start | bytes 18440 | tf_op jit(solution)/shard_map/ppermute | solution.py:28
  13.1 34.7 %copy-start.10 = (f32[128,5,1]{0,1,2:T(8,128)S(1)}, f32[128,5,1]{0,1,2:T(8,128)}, u32[]{:S(2)}) copy-start(f32[128,5,1]{0,1,2:T(8,128)} %constant.534) | copy-start | bytes 7684
  47.7 1.8 copy-start.9
  51.4 18.4 %copy-start.2 = (f32[128]{0:T(128)S(1)}, f32[128]{0:T(128)}, u32[]{:S(2)}) copy-start(f32[128]{0:T(128)} %constant.2011) | copy-start | bytes 1540
  51.4 18.4 %copy-start.4 = (f32[128]{0:T(128)S(1)}, f32[128]{0:T(128)}, u32[]{:S(2)}) copy-start(f32[128]{0:T(128)} %constant.489.clone..sunk.15) | copy-start | bytes 1540
  51.4 18.4 %copy-start.5 = (f32[128]{0:T(128)S(1)}, f32[128]{0:T(128)}, u32[]{:S(2)}) copy-start(f32[128]{0:T(128)} %constant.2010) | copy-start | bytes 1540
  51.4 18.4 %copy-start.6 = (f32[128]{0:T(128)S(1)}, f32[128]{0:T(128)}, u32[]{:S(2)}) copy-start(f32[128]{0:T(128)} %constant.490.clone..sunk.15) | copy-start | bytes 1540
  51.4 18.4 %copy-start.7 = (f32[128]{0:T(128)S(1)}, f32[128]{0:T(128)}, u32[]{:S(2)}) copy-start(f32[128]{0:T(128)} %constant.2009) | copy-start | bytes 1540
  69.9 13.5 %copy-start = (s32[16,9]{1,0:T(8,128)S(1)}, s32[16,9]{1,0:T(8,128)}, u32[]{:S(2)}) copy-start(s32[16,9]{1,0:T(8,128)} %param.28) | copy-start | bytes 1732
  69.9 13.8 %copy-start.1 = (f32[2048]{0:T(1024)S(1)}, f32[2048]{0:T(1024)}, u32[]{:S(2)}) copy-start(f32[2048]{0:T(1024)} %param.25) | copy-start | bytes 24580
  69.9 14.0 %copy-start.3 = (f32[3,2048]{1,0:T(4,128)S(1)}, f32[3,2048]{1,0:T(4,128)}, u32[]{:S(2)}) copy-start(f32[3,2048]{1,0:T(4,128)} %param.24) | copy-start | bytes 73732
  153.1 34.8 %collective-permute-start.4 = (f32[3,512]{1,0:T(4,128)S(1)}, f32[3,512]{1,0:T(4,128)S(1)}, u32[]{:S(2)}, u32[]{:S(2)}) collective-permute-start(f32[3,512]{1,0:T(4,128)S(1)} %get-tuple-element.1077), channel_id=1, source_target_pairs={{0,1},{1,2},{2,3},{3,4},{4,5},{5,6},{6,7},{7,8},{8,9},{9,10},{10,1... | collective-permute-start | bytes 18440 | tf_op jit(solution)/shard_map/ppermute | solution.py:26
  153.2 34.8 %collective-permute-start.5 = (f32[3,512]{1,0:T(4,128)S(1)}, f32[3,512]{1,0:T(4,128)S(1)}, u32[]{:S(2)}, u32[]{:S(2)}) collective-permute-start(f32[3,512]{1,0:T(4,128)S(1)} %get-tuple-element.1078), channel_id=1, source_target_pairs={{1,0},{2,1},{3,2},{4,3},{5,4},{6,5},{7,6},{8,7},{9,8},{10,9},{11,1... | collective-permute-start | bytes 18440 | tf_op jit(solution)/shard_map/ppermute | solution.py:28
  321.2 34.8 %collective-permute-start.6 = (f32[3,512]{1,0:T(4,128)S(1)}, f32[3,512]{1,0:T(4,128)S(1)}, u32[]{:S(2)}, u32[]{:S(2)}) collective-permute-start(f32[3,512]{1,0:T(4,128)S(1)} %get-tuple-element.1069), channel_id=1, source_target_pairs={{0,1},{1,2},{2,3},{3,4},{4,5},{5,6},{6,7},{7,8},{8,9},{9,10},{10,1... | collective-permute-start | bytes 18440 | tf_op jit(solution)/shard_map/ppermute | solution.py:26
  321.3 34.8 %collective-permute-start.7 = (f32[3,512]{1,0:T(4,128)S(1)}, f32[3,512]{1,0:T(4,128)S(1)}, u32[]{:S(2)}, u32[]{:S(2)}) collective-permute-start(f32[3,512]{1,0:T(4,128)S(1)} %get-tuple-element.1070), channel_id=1, source_target_pairs={{1,0},{2,1},{3,2},{4,3},{5,4},{6,5},{7,6},{8,7},{9,8},{10,9},{11,1... | collective-permute-start | bytes 18440 | tf_op jit(solution)/shard_map/ppermute | solution.py:28
where the time goes:
time: 434 us; the launch traced here: 428 us
  blocking collectives  237 us (55%)
  other arithmetic  145 us (33%)
  starting transfers between devices  19 us (4%)
  matrix products  13.6 us (3%)
  between operations  5.61 us (1%)
    reduce_sum x24, other arithmetic, near_tiles(): jnp.sum(weighted * delta_x - coef_three * moments[0][:, None, :], axis=2)  106 us
    psum x3, blocking collectives, moment(): return lax.psum(jnp.sum(values, axis=1), ('blk', 'oct', 'sub'))  90.8 us
    psum x2, blocking collectives, squares(): return lax.psum(jnp.sum(resid * scaled), ('blk', 'oct', 'sub'))  62.2 us
    all_gather x3, blocking collectives, induced(): piece = lax.all_gather(weights, ('blk', 'oct', 'sub'), axis=0, tiled=True)  52.3 us
    psum x1, blocking collectives, on_device(): lax.psum(jnp.sum(direction * image), ('blk', 'oct', 'sub'))  32 us
    reduce_sum x6, other arithmetic, far_block(): field_x = jnp.sum(weighted * delta_x - coef_three * weight_x, axis=(2, 3))  28.8 us
    ppermute x4, starting transfers between devices, padded(): lax.ppermute(head, axis, [((i + 1) % count, i) for i in range(count)])  18.3 us
  transfers between devices with their start and end apart: 8, of which 0 were waited for; matrix products, arithmetic and copies ran while one was open for 11% of the time, Pallas kernels for 0%

commit v1 on v0

--- a/solution.py
+++ b/solution.py
@@ -207,7 +207,7 @@
         return near + far - surface * total[:, None]
 
     def moment(values):
-        return lax.psum(jnp.sum(values, axis=1), ("blk", "oct", "sub"))
+        return jnp.sum(lax.all_gather(jnp.sum(values, axis=1), ("blk", "oct", "sub")), axis=0)
 
     def squares(resid, scaled):
         return lax.psum(jnp.sum(resid * scaled), ("blk", "oct", "sub"))

time: 434 us -> 438 us (level)
    psum x3 -> x0, blocking collectives: 90.8 us -> none  [moment(): return lax.psum(jnp.sum(values, axis=1), ('blk', 'oct', 'sub'))]
    unnamed x0 -> x3, blocking collectives: none -> 90.7 us
where the time goes in v1:
time: 438 us; the launch traced here: 431 us
  blocking collectives  237 us (54%)
  other arithmetic  145 us (33%)
  starting transfers between devices  19 us (4%)
  matrix products  13.7 us (3%)
  local copies, waits for them, and re-layouts  6.48 us (1%)
  between operations  6.07 us (1%)
    reduce_sum x24, other arithmetic, near_tiles(): jnp.sum(weighted * delta_x - coef_three * moments[0][:, None, :], axis=2)  106 us
    unnamed x3, blocking collectives  90.7 us
    psum x2, blocking collectives, squares(): return lax.psum(jnp.sum(resid * scaled), ('blk', 'oct', 'sub'))  62.2 us
    all_gather x3, blocking collectives, induced(): piece = lax.all_gather(weights, ('blk', 'oct', 'sub'), axis=0, tiled=True)  52.3 us
    psum x1, blocking collectives, on_device(): lax.psum(jnp.sum(direction * image), ('blk', 'oct', 'sub'))  32 us
    reduce_sum x6, other arithmetic, far_block(): field_x = jnp.sum(weighted * delta_x - coef_three * weight_x, axis=(2, 3))  28.8 us
    ppermute x4, starting transfers between devices, padded(): lax.ppermute(head, axis, [((i + 1) % count, i) for i in range(count)])  18.3 us
  transfers between devices with their start and end apart: 8, of which 0 were waited for; matrix products, arithmetic and copies ran while one was open for 11% of the time, Pallas kernels for 0%

profile of v1, /device:TPU:0, one launch (start us, length us, event | category | flops | bytes accessed | tf_op | source)
XLA Modules:
  0.0 431.4 jit_solution(7909577379564054714)
XLA Ops:
  2.6 5.0 %collective-permute-start.2 = (f32[5,512]{1,0:T(8,128)S(1)}, f32[5,512]{1,0:T(8,128)S(1)}, u32[]{:S(2)}, u32[]{:S(2)}) collective-permute-start(f32[5,512]{1,0:T(8,128)S(1)} %get-tuple-element.990), channel_id=1, source_target_pairs={{1,0},{2,1},{3,2},{4,3},{5,4},{6,5},{7,6},{8,7},{9,8},{10,9},{11,1... | collective-permute-start | bytes 30728 | tf_op jit(solution)/shard_map/ppermute | solution.py:28
  8.6 4.4 %collective-permute-start.3 = (f32[3,512]{1,0:T(4,128)S(1)}, f32[3,512]{1,0:T(4,128)S(1)}, u32[]{:S(2)}, u32[]{:S(2)}) collective-permute-start(f32[3,512]{1,0:T(4,128)S(1)} %get-tuple-element.1086), channel_id=1, source_target_pairs={{1,0},{2,1},{3,2},{4,3},{5,4},{6,5},{7,6},{8,7},{9,8},{10,9},{11,1... | collective-permute-start | bytes 18440 | tf_op jit(solution)/shard_map/ppermute | solution.py:28
  16.1 29.5 %all-reduce = f32[48]{0:T(128)S(1)} all-reduce(f32[48]{0:T(128)S(1)} %dynamic-update-slice), channel_id=2, replica_groups=mesh['groups'=2,'blk'=4,'oct'=2,'sub'=2] {'blk','oct','sub'}, use_global_device_ids=true, to_apply=%add | all-reduce | flops 48 | bytes 384
  50.0 1.8 convolution_multiply_fusion.1
  51.8 1.8 fusion.90
  54.3 17.8 %all_gather.27 = f32[32,3,128]{2,1,0:T(4,128)S(1)} all-gather(f32[2,3,128]{2,1,0:T(4,128)S(1)} %fusion.782), channel_id=1, replica_groups=mesh['groups'=2,'blk'=4,'oct'=2,'sub'=2] {'blk','oct','sub'}, dimensions={0}, use_global_device_ids=true | all-gather | bytes 52224 | tf_op jit(solution)/shard_map/all_gather | solution.py:192
  72.1 13.5 %while.51 = (s32[]{:T(128)}, f32[2,3,128]{2,0,1:T(2,128)S(1)}, s32[2]{0:T(128)S(1)}, f32[2,16,3,128]{3,1,2,0:T(8,128)S(1)}, s32[]{:T(128)}, /*index=5*/s32[]{:T(...) while((s32[]{:T(128)}, f32[2,3,128]{2,0,1:T(2,128)S(1)}, ...), condition=%wide.region_31.32_spmd.clone.clone.clone.clone, body=%wide.region_27.31_spmd.sunk.clone.clone.clone.clone.sunk | while | flops 16765948 | bytes 2795035 | solution.py:203
  74.1 4.8 %subtract_reduce_fusion.9 = (f32[2,128]{1,0:T(2,128)S(1)}, f32[2,128]{1,0:T(2,128)S(1)}, f32[2,128]{1,0:T(2,128)S(1)}) fusion(f32[16,128]{1,0:T(8,128)S(1)} %get-tuple-element.1216, f32[128,128]{1,0:T(8,128)S(1)} %get-tuple-element.1217, pred[2,16]{1,0:T(4,128)(4,1)S(1)} %fusion.814, f32[16,128]{1,0:T(8,128)S(1)} %broadcast_add_fusion.12, ...), kind=kLoop, calls=%fused_computation.28.clone.1 | loop fusion | flops 15727872 | bytes 1282080 | tf_op jit(solution)/shard_map/while/body/eval_jaxpr/reduce_sum | solution.py:163
  80.8 4.8 %subtract_reduce_fusion.9 = (f32[2,128]{1,0:T(2,128)S(1)}, f32[2,128]{1,0:T(2,128)S(1)}, f32[2,128]{1,0:T(2,128)S(1)}) fusion(f32[16,128]{1,0:T(8,128)S(1)} %get-tuple-element.1216, f32[128,128]{1,0:T(8,128)S(1)} %get-tuple-element.1217, pred[2,16]{1,0:T(4,128)(4,1)S(1)} %fusion.814, f32[16,128]{1,0:T(8,128)S(1)} %broadcast_add_fusion.12, ...), kind=kLoop, calls=%fused_computation.28.clone.1 | loop fusion | flops 15727872 | bytes 1282080 | tf_op jit(solution)/shard_map/while/body/eval_jaxpr/reduce_sum | solution.py:163
  86.4 4.0 fusion.558
  90.5 4.0 fusion.585
  94.5 4.0 fusion.567
  98.5 4.0 fusion.576
  102.5 4.0 fusion.603
  106.5 4.0 fusion.621
  110.5 4.0 fusion.612
  114.5 7.3 %fusion.630 = (f32[16,128]{1,0:T(8,128)S(1)}, f32[16,128]{1,0:T(8,128)S(1)}, f32[16,128]{1,0:T(8,128)S(1)}, f32[16,128]{1,0:T(8,128)S(1)}, f32[16,128]{1,0:T(8,128)S(1)}, /*index=5*/f32[16,128]{1,0:T(8,128)S(1)}) fusion(f32[16,128]{1,0:T(8,128)S(1)} %bitcast.841, f32[16,128]{1,0:T(8,128)S(1)} %bitcast.736, f32[16,128]{1,0:T(8,128)S(1)} %bitcast.932, ...), kind=kLoop, calls=%fused_computation.815 | loop fusion | flops 30920704 | bytes 180256 | tf_op jit(solution)/shard_map/reduce_sum | solution.py:70
  123.2 31.6 %all-reduce.1 = f32[48]{0:T(128)S(1)} all-reduce(f32[48]{0:T(128)S(1)} %dynamic-update-slice.1), channel_id=3, replica_groups=mesh['groups'=2,'blk'=4,'oct'=2,'sub'=2] {'blk','oct','sub'}, use_global_device_ids=true, to_apply=%add.1 | all-reduce | flops 48 | bytes 384
  155.8 4.4 %collective-permute-start.5 = (f32[3,512]{1,0:T(4,128)S(1)}, f32[3,512]{1,0:T(4,128)S(1)}, u32[]{:S(2)}, u32[]{:S(2)}) collective-permute-start(f32[3,512]{1,0:T(4,128)S(1)} %get-tuple-element.1078), channel_id=1, source_target_pairs={{1,0},{2,1},{3,2},{4,3},{5,4},{6,5},{7,6},{8,7},{9,8},{10,9},{11,1... | collective-permute-start | bytes 18440 | tf_op jit(solution)/shard_map/ppermute | solution.py:28
  160.2 17.3 %all_gather.30 = f32[32,3,128]{2,1,0:T(4,128)S(1)} all-gather(f32[2,3,128]{2,1,0:T(4,128)S(1)} %fusion.684), channel_id=1, replica_groups=mesh['groups'=2,'blk'=4,'oct'=2,'sub'=2] {'blk','oct','sub'}, dimensions={0}, use_global_device_ids=true | all-gather | bytes 52224 | tf_op jit(solution)/shard_map/all_gather | solution.py:192
  177.5 13.0 %while.52 = (s32[]{:T(128)}, f32[2,3,128]{2,0,1:T(2,128)S(1)}, s32[2]{0:T(128)S(1)}, f32[2,16,3,128]{3,1,2,0:T(8,128)S(1)}, s32[]{:T(128)}, /*index=5*/s32[]{:T(...) while((s32[]{:T(128)}, f32[2,3,128]{2,0,1:T(2,128)S(1)}, ...), condition=%wide.region_67.68_spmd.clone.clone.clone.clone, body=%wide.region_63.67_spmd.sunk.clone.clone.clone.clone.sunk | while | flops 16765948 | bytes 2795035 | solution.py:203
  179.2 4.8 %subtract_reduce_fusion.10 = (f32[2,128]{1,0:T(2,128)S(1)}, f32[2,128]{1,0:T(2,128)S(1)}, f32[2,128]{1,0:T(2,128)S(1)}) fusion(f32[16,128]{1,0:T(8,128)S(1)} %get-tuple-element.1230, f32[128,128]{1,0:T(8,128)S(1)} %get-tuple-element.1231, pred[2,16]{1,0:T(4,128)(4,1)S(1)} %fusion.817, f32[16,128]{1,0:T(8,128)S(1)} %broadcast_add_fusion.14, ...), kind=kLoop, calls=%fused_computation.82.clone.1 | loop fusion | flops 15727872 | bytes 1282080 | tf_op jit(solution)/shard_map/while/body/eval_jaxpr/reduce_sum | solution.py:163
  185.7 4.8 %subtract_reduce_fusion.10 = (f32[2,128]{1,0:T(2,128)S(1)}, f32[2,128]{1,0:T(2,128)S(1)}, f32[2,128]{1,0:T(2,128)S(1)}) fusion(f32[16,128]{1,0:T(8,128)S(1)} %get-tuple-element.1230, f32[128,128]{1,0:T(8,128)S(1)} %get-tuple-element.1231, pred[2,16]{1,0:T(4,128)(4,1)S(1)} %fusion.817, f32[16,128]{1,0:T(8,128)S(1)} %broadcast_add_fusion.14, ...), kind=kLoop, calls=%fused_computation.82.clone.1 | loop fusion | flops 15727872 | bytes 1282080 | tf_op jit(solution)/shard_map/while/body/eval_jaxpr/reduce_sum | solution.py:163
  190.6 4.0 fusion.602
  194.7 4.0 fusion.575
  198.7 4.0 fusion.566
  202.7 4.0 fusion.557
  206.7 4.0 fusion.584
  210.8 4.0 fusion.611
  214.8 4.0 fusion.620
  218.8 7.3 %fusion.629 = (f32[16,128]{1,0:T(8,128)S(1)}, f32[16,128]{1,0:T(8,128)S(1)}, f32[16,128]{1,0:T(8,128)S(1)}, f32[16,128]{1,0:T(8,128)S(1)}, f32[16,128]{1,0:T(8,128)S(1)}, /*index=5*/f32[16,128]{1,0:T(8,128)S(1)}) fusion(f32[16,128]{1,0:T(8,128)S(1)} %bitcast.873, f32[16,128]{1,0:T(8,128)S(1)} %bitcast.737, f32[16,128]{1,0:T(8,128)S(1)} %bitcast.940, ...), kind=kLoop, calls=%fused_computation.814 | loop fusion | flops 30920704 | bytes 180256 | tf_op jit(solution)/shard_map/reduce_sum | solution.py:70
  227.8 32.1 %all-reduce.3 = (f32[]{:T(128)}, f32[]{:T(128)}) all-reduce(f32[]{:T(128)} %get-tuple-element.870, f32[]{:T(128)} %get-tuple-element.869), channel_id=1, replica_groups=mesh['groups'=2,'blk'=4,'oct'=2,'sub'=2] {'blk','oct','sub'}, use_global_device_ids=true, to_apply=%region_35.36 | all-reduce | flops 2 | bytes 16 | tf_op jit(solution)/shard_map/psum | solution.py:213
  261.8 30.1 %psum.30 = f32[]{:T(128)} all-reduce(f32[]{:T(128)} %fusion.632), channel_id=1, replica_groups=mesh['groups'=2,'blk'=4,'oct'=2,'sub'=2] {'blk','oct','sub'}, use_global_device_ids=true, to_apply=%region_73.74 | all-reduce | flops 1 | bytes 8 | tf_op jit(solution)/shard_map/psum | solution.py:213
  293.5 29.7 %all-reduce.2 = f32[48]{0:T(128)S(1)} all-reduce(f32[48]{0:T(128)S(1)} %dynamic-update-slice.2), channel_id=4, replica_groups=mesh['groups'=2,'blk'=4,'oct'=2,'sub'=2] {'blk','oct','sub'}, use_global_device_ids=true, to_apply=%add.2 | all-reduce | flops 48 | bytes 384
  324.2 4.4 %collective-permute-start.7 = (f32[3,512]{1,0:T(4,128)S(1)}, f32[3,512]{1,0:T(4,128)S(1)}, u32[]{:S(2)}, u32[]{:S(2)}) collective-permute-start(f32[3,512]{1,0:T(4,128)S(1)} %get-tuple-element.1070), channel_id=1, source_target_pairs={{1,0},{2,1},{3,2},{4,3},{5,4},{6,5},{7,6},{8,7},{9,8},{10,9},{11,1... | collective-permute-start | bytes 18440 | tf_op jit(solution)/shard_map/ppermute | solution.py:28
  328.6 17.3 %all_gather.33 = f32[32,3,128]{2,1,0:T(4,128)S(1)} all-gather(f32[2,3,128]{2,1,0:T(4,128)S(1)} %fusion.783), channel_id=1, replica_groups=mesh['groups'=2,'blk'=4,'oct'=2,'sub'=2] {'blk','oct','sub'}, dimensions={0}, use_global_device_ids=true | all-gather | bytes 52224 | tf_op jit(solution)/shard_map/all_gather | solution.py:192
  345.9 13.2 %while.53 = (s32[]{:T(128)}, f32[2,3,128]{2,0,1:T(2,128)S(1)}, s32[2]{0:T(128)S(1)}, f32[2,16,3,128]{3,1,2,0:T(8,128)S(1)}, s32[]{:T(128)}, /*index=5*/s32[]{:T(...) while((s32[]{:T(128)}, f32[2,3,128]{2,0,1:T(2,128)S(1)}, ...), condition=%wide.region_105.106_spmd.clone.clone.clone.clone, body=%wide.region_101.105_spmd.sunk.clone.clone.clone.clone.sunk | while | flops 16765948 | bytes 2795035 | solution.py:203
  347.7 4.8 %subtract_reduce_fusion.11 = (f32[2,128]{1,0:T(2,128)S(1)}, f32[2,128]{1,0:T(2,128)S(1)}, f32[2,128]{1,0:T(2,128)S(1)}) fusion(f32[16,128]{1,0:T(8,128)S(1)} %get-tuple-element.1244, f32[128,128]{1,0:T(8,128)S(1)} %get-tuple-element.1245, pred[2,16]{1,0:T(4,128)(4,1)S(1)} %fusion.820, f32[16,128]{1,0:T(8,128)S(1)} %broadcast_add_fusion.16, ...), kind=kLoop, calls=%fused_computation.136.clone.1 | loop fusion | flops 15727872 | bytes 1282080 | tf_op jit(solution)/shard_map/while/body/eval_jaxpr/reduce_sum | solution.py:163
  354.3 4.8 %subtract_reduce_fusion.11 = (f32[2,128]{1,0:T(2,128)S(1)}, f32[2,128]{1,0:T(2,128)S(1)}, f32[2,128]{1,0:T(2,128)S(1)}) fusion(f32[16,128]{1,0:T(8,128)S(1)} %get-tuple-element.1244, f32[128,128]{1,0:T(8,128)S(1)} %get-tuple-element.1245, pred[2,16]{1,0:T(4,128)(4,1)S(1)} %fusion.820, f32[16,128]{1,0:T(8,128)S(1)} %broadcast_add_fusion.16, ...), kind=kLoop, calls=%fused_computation.136.clone.1 | loop fusion | flops 15727872 | bytes 1282080 | tf_op jit(solution)/shard_map/while/body/eval_jaxpr/reduce_sum | solution.py:163
  359.2 4.0 fusion.556
  363.3 4.0 fusion.601
  367.3 4.0 fusion.565
  371.3 4.0 fusion.574
  375.3 4.0 fusion.583
  379.4 4.0 fusion.610
  383.4 4.0 fusion.619
  387.4 7.3 %fusion.628 = (f32[16,128]{1,0:T(8,128)S(1)}, f32[16,128]{1,0:T(8,128)S(1)}, f32[16,128]{1,0:T(8,128)S(1)}, f32[16,128]{1,0:T(8,128)S(1)}, f32[16,128]{1,0:T(8,128)S(1)}, /*index=5*/f32[16,128]{1,0:T(8,128)S(1)}) fusion(f32[16,128]{1,0:T(8,128)S(1)} %bitcast.863, f32[16,128]{1,0:T(8,128)S(1)} %bitcast.738, f32[16,128]{1,0:T(8,128)S(1)} %bitcast.948, ...), kind=kLoop, calls=%fused_computation.813 | loop fusion | flops 30920704 | bytes 180256 | tf_op jit(solution)/shard_map/reduce_sum | solution.py:70
  396.4 32.0 %psum.31 = f32[]{:T(128)} all-reduce(f32[]{:T(128)} %get-tuple-element.1104), channel_id=1, replica_groups=mesh['groups'=2,'blk'=4,'oct'=2,'sub'=2] {'blk','oct','sub'}, use_global_device_ids=true, to_apply=%region_109.110 | all-reduce | flops 1 | bytes 8 | tf_op jit(solution)/shard_map/psum | solution.py:222
  (187 shorter events, 27.3 us)
Async XLA Ops:
  0.6 47.3 %copy-start.8 = (f32[5,5,1]{1,0,2:T(8,128)S(1)}, f32[5,5,1]{1,0,2:T(8,128)}, u32[]{:S(2)}) copy-start(f32[5,5,1]{1,0,2:T(8,128)} %constant.550) | copy-start | bytes 304
  0.6 47.5 %copy-start.11 = (f32[128,5,1]{0,1,2:T(8,128)S(1)}, f32[128,5,1]{0,1,2:T(8,128)}, u32[]{:S(2)}) copy-start(f32[128,5,1]{0,1,2:T(8,128)} %constant.551) | copy-start | bytes 7684
  2.1 84.0 %collective-permute-start = (f32[5,512]{1,0:T(8,128)S(1)}, f32[5,512]{1,0:T(8,128)S(1)}, u32[]{:S(2)}, u32[]{:S(2)}) collective-permute-start(f32[5,512]{1,0:T(8,128)S(1)} %get-tuple-element.989), channel_id=1, source_target_pairs={{0,1},{1,2},{2,3},{3,4},{4,5},{5,6},{6,7},{7,8},{8,9},{9,10},{10,1... | collective-permute-start | bytes 30728 | tf_op jit(solution)/shard_map/ppermute | solution.py:26
  2.6 83.5 %collective-permute-start.2 = (f32[5,512]{1,0:T(8,128)S(1)}, f32[5,512]{1,0:T(8,128)S(1)}, u32[]{:S(2)}, u32[]{:S(2)}) collective-permute-start(f32[5,512]{1,0:T(8,128)S(1)} %get-tuple-element.990), channel_id=1, source_target_pairs={{1,0},{2,1},{3,2},{4,3},{5,4},{6,5},{7,6},{8,7},{9,8},{10,9},{11,1... | collective-permute-start | bytes 30728 | tf_op jit(solution)/shard_map/ppermute | solution.py:28
  8.6 77.4 %collective-permute-start.1 = (f32[3,512]{1,0:T(4,128)S(1)}, f32[3,512]{1,0:T(4,128)S(1)}, u32[]{:S(2)}, u32[]{:S(2)}) collective-permute-start(f32[3,512]{1,0:T(4,128)S(1)} %get-tuple-element.1085), channel_id=1, source_target_pairs={{0,1},{1,2},{2,3},{3,4},{4,5},{5,6},{6,7},{7,8},{8,9},{9,10},{10,1... | collective-permute-start | bytes 18440 | tf_op jit(solution)/shard_map/ppermute | solution.py:26
  8.6 77.4 %collective-permute-start.3 = (f32[3,512]{1,0:T(4,128)S(1)}, f32[3,512]{1,0:T(4,128)S(1)}, u32[]{:S(2)}, u32[]{:S(2)}) collective-permute-start(f32[3,512]{1,0:T(4,128)S(1)} %get-tuple-element.1086), channel_id=1, source_target_pairs={{1,0},{2,1},{3,2},{4,3},{5,4},{6,5},{7,6},{8,7},{9,8},{10,9},{11,1... | collective-permute-start | bytes 18440 | tf_op jit(solution)/shard_map/ppermute | solution.py:28
  13.1 36.9 %copy-start.10 = (f32[128,5,1]{0,1,2:T(8,128)S(1)}, f32[128,5,1]{0,1,2:T(8,128)}, u32[]{:S(2)}) copy-start(f32[128,5,1]{0,1,2:T(8,128)} %constant.552) | copy-start | bytes 7684
  50.0 1.8 copy-start.9
  53.6 18.4 %copy-start.2 = (f32[128]{0:T(128)S(1)}, f32[128]{0:T(128)}, u32[]{:S(2)}) copy-start(f32[128]{0:T(128)} %constant.2029) | copy-start | bytes 1540
  53.6 18.4 %copy-start.4 = (f32[128]{0:T(128)S(1)}, f32[128]{0:T(128)}, u32[]{:S(2)}) copy-start(f32[128]{0:T(128)} %constant.489.clone..sunk.15) | copy-start | bytes 1540
  53.7 18.4 %copy-start.5 = (f32[128]{0:T(128)S(1)}, f32[128]{0:T(128)}, u32[]{:S(2)}) copy-start(f32[128]{0:T(128)} %constant.2028) | copy-start | bytes 1540
  53.7 18.4 %copy-start.6 = (f32[128]{0:T(128)S(1)}, f32[128]{0:T(128)}, u32[]{:S(2)}) copy-start(f32[128]{0:T(128)} %constant.490.clone..sunk.15) | copy-start | bytes 1540
  53.7 18.4 %copy-start.7 = (f32[128]{0:T(128)S(1)}, f32[128]{0:T(128)}, u32[]{:S(2)}) copy-start(f32[128]{0:T(128)} %constant.2027) | copy-start | bytes 1540
  72.1 13.5 %copy-start = (s32[16,9]{1,0:T(8,128)S(1)}, s32[16,9]{1,0:T(8,128)}, u32[]{:S(2)}) copy-start(s32[16,9]{1,0:T(8,128)} %param.28) | copy-start | bytes 1732
  72.1 13.8 %copy-start.1 = (f32[2048]{0:T(1024)S(1)}, f32[2048]{0:T(1024)}, u32[]{:S(2)}) copy-start(f32[2048]{0:T(1024)} %param.25) | copy-start | bytes 24580
  72.1 14.0 %copy-start.3 = (f32[3,2048]{1,0:T(4,128)S(1)}, f32[3,2048]{1,0:T(4,128)}, u32[]{:S(2)}) copy-start(f32[3,2048]{1,0:T(4,128)} %param.24) | copy-start | bytes 73732
  155.7 34.8 %collective-permute-start.4 = (f32[3,512]{1,0:T(4,128)S(1)}, f32[3,512]{1,0:T(4,128)S(1)}, u32[]{:S(2)}, u32[]{:S(2)}) collective-permute-start(f32[3,512]{1,0:T(4,128)S(1)} %get-tuple-element.1077), channel_id=1, source_target_pairs={{0,1},{1,2},{2,3},{3,4},{4,5},{5,6},{6,7},{7,8},{8,9},{9,10},{10,1... | collective-permute-start | bytes 18440 | tf_op jit(solution)/shard_map/ppermute | solution.py:26
  155.8 34.8 %collective-permute-start.5 = (f32[3,512]{1,0:T(4,128)S(1)}, f32[3,512]{1,0:T(4,128)S(1)}, u32[]{:S(2)}, u32[]{:S(2)}) collective-permute-start(f32[3,512]{1,0:T(4,128)S(1)} %get-tuple-element.1078), channel_id=1, source_target_pairs={{1,0},{2,1},{3,2},{4,3},{5,4},{6,5},{7,6},{8,7},{9,8},{10,9},{11,1... | collective-permute-start | bytes 18440 | tf_op jit(solution)/shard_map/ppermute | solution.py:28
  324.2 35.0 %collective-permute-start.6 = (f32[3,512]{1,0:T(4,128)S(1)}, f32[3,512]{1,0:T(4,128)S(1)}, u32[]{:S(2)}, u32[]{:S(2)}) collective-permute-start(f32[3,512]{1,0:T(4,128)S(1)} %get-tuple-element.1069), channel_id=1, source_target_pairs={{0,1},{1,2},{2,3},{3,4},{4,5},{5,6},{6,7},{7,8},{8,9},{9,10},{10,1... | collective-permute-start | bytes 18440 | tf_op jit(solution)/shard_map/ppermute | solution.py:26
  324.2 35.0 %collective-permute-start.7 = (f32[3,512]{1,0:T(4,128)S(1)}, f32[3,512]{1,0:T(4,128)S(1)}, u32[]{:S(2)}, u32[]{:S(2)}) collective-permute-start(f32[3,512]{1,0:T(4,128)S(1)} %get-tuple-element.1070), channel_id=1, source_target_pairs={{1,0},{2,1},{3,2},{4,3},{5,4},{6,5},{7,6},{8,7},{9,8},{10,9},{11,1... | collective-permute-start | bytes 18440 | tf_op jit(solution)/shard_map/ppermute | solution.py:28
